TPU v7x, 256 devices: a whole 4x4x8 slice. The times are simulated.
256 devices in a mesh: head: 16 (over z, core), tail: 16 (over y, x).
Axes of the slice: x: 4, y: 4, z: 8, core: 2. Of those that a mesh axis runs over, the one named last changes fastest.
Arguments:
- head_emb: bfloat16 [131072, 800], P(('head', 'tail')), may hold values from -48 to 48
- head_state: float32 [131072], P(('head', 'tail')), may hold values from 0.01 to 1
- tail_emb: bfloat16 [64, 128, 800], P('tail'), may hold values from -1.5 to 1.5
- tail_state: float32 [64, 128], P('tail'), may hold values from 0.01 to 1
- relation_emb: bfloat16 [1024, 800], replicated, may hold values from -3.5 to 3.5
- head_rows: int32 [1024, 256], P(('head', 'tail')), may hold values from 0 to 511
- relations: int32 [1024, 256], P(('head', 'tail')), may hold values from 0 to 1023
- tail_offsets: int32 [1024, 256], P(('head', 'tail')), may hold values from 0 to 127
- tail_owner: int32 [1024, 1], P(('head', 'tail')), may hold values from 0 to 15; in each aligned block of 4 rows (0 to 3, 4 to 7, ...) at most 2 rows name the same one
- tail_local: int32 [1024], P(('head', 'tail')), may hold values from 0 to 3
- block_count: int32 [256], P(('head', 'tail')), may hold values from 1 to 4, as said below
- neg_blocks: int32 [8], replicated, may hold values from 0 to 63, as said below
Outputs:
- head_new: bfloat16 [131072, 800], P(('head', 'tail'))
- head_state_new: float32 [131072], P(('head', 'tail'))
- tail_new: bfloat16 [64, 128, 800], P('tail')
- tail_state_new: float32 [64, 128], P('tail')
Inputs may be any that keep to these rules, and one draw needn't show every extreme that they name: `tail_owner`: no tail index owns the tail blocks of more than 2 edge block slots of one device, and in some devices one owns exactly 2. `block_count`: some device has all 4 slots live. `neg_blocks`: distinct tail blocks; the last tail block is always among them.
All inputs are finite; a program needn't handle non-finite values.
Results may differ from a plain program's by a relative error of at most 0.0012.
The roundings to bfloat16 on the way count: a program that leaves them out, or rounds other values in their place, can miss the bound.
Values may be sent and summed in bfloat16 or wider, within the bound.
A program may use at most 128 MiB of HBM per device.

v0:
```python
import math
import jax
import jax.numpy as jnp
from jax import lax
from jax.sharding import PartitionSpec as P

LEARN_RATE = 0.3


def complex_product(left, right):
    half_width = left.shape[-1] // 2
    left_re, left_im = (left[..., :half_width], left[..., half_width:])
    right_re, right_im = (right[..., :half_width], right[..., half_width:])
    return jnp.concatenate(
        [left_re * right_re - left_im * right_im, left_re * right_im + left_im * right_re], axis=-1
    )


def conj_product(left, right):
    half_width = left.shape[-1] // 2
    left_re, left_im = (left[..., :half_width], left[..., half_width:])
    right_re, right_im = (right[..., :half_width], right[..., half_width:])
    return jnp.concatenate(
        [left_re * right_re + left_im * right_im, left_im * right_re - left_re * right_im], axis=-1
    )


def row_adagrad(embedding, adagrad_state, gradient):
    state_next = adagrad_state + jnp.mean(gradient * gradient, axis=-1)
    updated = (
        embedding.astype(jnp.float32) - LEARN_RATE * gradient / jnp.sqrt(state_next)[..., None]
    )
    return (updated.astype(jnp.bfloat16), state_next)


def head_sum(tail_grad):
    return lax.psum(tail_grad, "head")


def per_device(
    head_emb,
    head_state,
    tail_emb,
    tail_state,
    relation_emb,
    head_rows,
    relations,
    tail_offsets,
    tail_owner,
    tail_local,
    block_count,
    neg_blocks,
):
    block_total = tail_local.shape[0]
    edge_count = head_rows.shape[1]
    row_width = head_emb.shape[1]
    span_rows = tail_emb.shape[1]
    owned_blocks = tail_emb.shape[0]
    peer_count = lax.axis_size("tail")
    tail_rank = lax.axis_index("tail")
    capacity = max(2, (2 * block_total + peer_count - 1) // peer_count)
    owner_rank = tail_owner[:, 0]
    positions = jnp.arange(block_total, dtype=jnp.int32)
    same_owner = owner_rank[:, None] == owner_rank[None, :]
    earlier = positions[None, :] < positions[:, None]
    slot_index = jnp.sum((same_owner & earlier).astype(jnp.int32), axis=1)
    slot_place = owner_rank * capacity + slot_index
    global_block = owner_rank * owned_blocks + tail_local
    partition = lax.all_gather(tail_emb, "tail", axis=0, tiled=True)
    chosen = jnp.take(partition, global_block, axis=0)
    mine_ids = neg_blocks - tail_rank * owned_blocks
    is_mine = (mine_ids >= 0) & (mine_ids < owned_blocks)
    own_negs = jnp.where(
        is_mine[:, None, None],
        jnp.take(tail_emb, jnp.clip(mine_ids, 0, owned_blocks - 1), axis=0),
        jnp.zeros((), jnp.bfloat16),
    )
    negatives = lax.psum(own_negs.astype(jnp.float32).astype(jnp.bfloat16), "tail").reshape(
        -1, row_width
    )
    total_edges = block_total * edge_count
    flat_rows = head_rows.reshape(-1)
    block_of = jnp.arange(total_edges, dtype=jnp.int32) // edge_count
    live_mask = (block_of < block_count[0]).astype(jnp.float32)
    tail_index = block_of * span_rows + tail_offsets.reshape(-1)
    tail_vectors = jnp.take(chosen.reshape(-1, row_width), tail_index, axis=0)
    relation_vectors = jnp.take(relation_emb, relations.reshape(-1), axis=0)
    head_vectors = jnp.take(head_emb, flat_rows, axis=0)
    query = complex_product(
        head_vectors.astype(jnp.float32), relation_vectors.astype(jnp.float32)
    ).astype(jnp.bfloat16)
    per_group = math.gcd(block_total, max(1, 512 // edge_count))
    group_rows = per_group * edge_count
    group_count = total_edges // group_rows

    def grouped(values):
        return values.reshape((group_count, group_rows) + values.shape[1:])

    def score_group(neg_total, group_items):
        query_rows, tail_rows, live_rows = group_items
        query_float = query_rows.astype(jnp.float32)
        positive = jnp.sum(query_float * tail_rows.astype(jnp.float32), axis=1)
        negative = lax.dot_general(
            query_rows, negatives, (((1,), (1,)), ((), ())), preferred_element_type=jnp.float32
        )
        largest = jnp.maximum(positive, jnp.max(negative, axis=1))
        pos_exp = jnp.exp(positive - largest)
        neg_exp = jnp.exp(negative - largest[:, None])
        denominator = pos_exp + jnp.sum(neg_exp, axis=1)
        pos_grad = (pos_exp / denominator - 1.0) * live_rows
        neg_grad = (neg_exp / denominator[:, None] * live_rows[:, None]).astype(jnp.bfloat16)
        query_grad = pos_grad[:, None] * tail_rows.astype(jnp.float32) + jnp.dot(
            neg_grad, negatives, preferred_element_type=jnp.float32
        )
        tail_part = pos_grad[:, None] * query_float
        neg_total = neg_total + lax.dot_general(
            neg_grad, query_rows, (((0,), (0,)), ((), ())), preferred_element_type=jnp.float32
        )
        return (neg_total, (query_grad, tail_part))

    neg_start = jnp.zeros((negatives.shape[0], row_width), jnp.float32)
    neg_part, (query_grad, tail_part) = lax.scan(
        score_group, neg_start, (grouped(query), grouped(tail_vectors), grouped(live_mask))
    )
    query_grad = query_grad.reshape(total_edges, row_width)
    tail_part = tail_part.reshape(total_edges, row_width)
    head_grad = (
        jnp.zeros(head_emb.shape, jnp.float32)
        .at[flat_rows]
        .add(conj_product(query_grad, relation_vectors.astype(jnp.float32)))
    )
    block_grad = (
        jnp.zeros((block_total * span_rows, row_width), jnp.float32)
        .at[tail_index]
        .add(tail_part)
        .astype(jnp.bfloat16)
    )
    outgoing = (
        jnp.zeros((peer_count * capacity, span_rows, row_width), jnp.bfloat16)
        .at[slot_place]
        .set(block_grad.reshape(block_total, span_rows, row_width))
    )
    outgoing = outgoing.reshape(peer_count, capacity, span_rows, row_width)
    slot_ids = (
        jnp.zeros((peer_count * capacity,), jnp.int32)
        .at[slot_place]
        .set(tail_local)
        .reshape(peer_count, capacity)
    )
    incoming, incoming_ids = (
        lax.all_to_all(outgoing, "tail", split_axis=0, concat_axis=0, tiled=True),
        lax.all_to_all(slot_ids, "tail", split_axis=0, concat_axis=0, tiled=True),
    )
    which_block = (
        incoming_ids.reshape(-1)[:, None] == jnp.arange(owned_blocks, dtype=jnp.int32)[None, :]
    ).astype(jnp.bfloat16)
    tail_grad = lax.dot_general(
        which_block,
        incoming.reshape(peer_count * capacity, span_rows * row_width),
        (((0,), (0,)), ((), ())),
        preferred_element_type=jnp.float32,
    )
    neg_weights = (
        (mine_ids[:, None] == jnp.arange(owned_blocks, dtype=jnp.int32)[None, :]) & is_mine[:, None]
    ).astype(jnp.float32)
    neg_all = lax.psum(neg_part, ("head", "tail"))
    tail_total = head_sum(tail_grad) + lax.dot_general(
        neg_weights,
        neg_all.reshape(neg_weights.shape[0], span_rows * row_width),
        (((0,), (0,)), ((), ())),
        precision=lax.Precision.HIGHEST,
        preferred_element_type=jnp.float32,
    )
    head_updated, head_state_updated = row_adagrad(head_emb, head_state, head_grad)
    tail_updated, tail_state_updated = row_adagrad(
        tail_emb, tail_state, tail_total.reshape(owned_blocks, span_rows, row_width)
    )
    return (head_updated, head_state_updated, tail_updated, tail_state_updated)


def solution(mesh):
    placed = (
        P(("head", "tail"), None),
        P(("head", "tail")),
        P("tail", None, None),
        P("tail", None),
        P(),
        P(("head", "tail"), None),
        P(("head", "tail"), None),
        P(("head", "tail"), None),
        P(("head", "tail"), None),
        P(("head", "tail")),
        P(("head", "tail")),
        P(),
    )
    return jax.shard_map(
        per_device,
        mesh=mesh,
        in_specs=placed,
        out_specs=(
            P(("head", "tail"), None),
            P(("head", "tail")),
            P("tail", None, None),
            P("tail", None),
        ),
        check_vma=False,
    )
```

profile of v0, /device:TPU:1, one launch (start us, length us, event | category | flops | bytes accessed | tf_op | source)
XLA Modules:
  0.0 729.9 jit_solution(752198037437776522)
XLA Ops:
  10.9 7.6 %all-to-all-start = ((s32[16,1,2]{2,1,0:T(1,128)}), s32[16,1,2]{2,1,0:T(1,128)S(1)}, u32[]{:S(2)}, u32[]{:S(2)}) async-start(s32[16,1,2]{2,1,0:T(1,128)} %bitcast.13), calls=%async_computation | async-start | bytes 16384 | tf_op jit(solution)/shard_map/all_to_all | solution.py:152
  20.1 1.4 select_select_fusion
  21.5 3.8 copy.82
  26.1 3.1 copy.79
  29.3 5.3 gather_fusion.3
  34.5 5.3 gather_fusion
  39.8 2.5 select_convert_fusion
  42.4 1.5 subtract_convert_fusion
  48.7 62.8 %all-gather.2.cloned.1.call-done = bf16[64,128,800]{1,2,0:T(8,128)(2,1)} async-done(((bf16[4,128,800]{1,2,0:T(8,128)(2,1)}), bf16[64,128,800]{1,2,0:T(8,128)(2,1)}) %all-gather.2.cloned.1.call-update) | async-done | bytes 13107216 | tf_op jit(solution)/shard_map/all_gather | solution.py:69
  111.5 5.4 gather_fusion.2
  119.6 5.3 gather_fusion.4
  124.9 3.3 broadcast_select_fusion
  128.2 3.5 copy.84
  131.6 81.5 %all-reduce.4.cloned.1.call-done = bf16[1024,800]{1,0:T(8,128)(2,1)} async-done(((bf16[1024,800]{1,0:T(8,128)(2,1)}), bf16[1024,800]{1,0:T(8,128)(2,1)}) %all-reduce.4.cloned.1.call-update) | async-done | bytes 1638416 | tf_op jit(solution)/shard_map/psum | solution.py:78
  213.2 30.7 %while.17 = (s32[]{:T(128)}, f32[1024,800]{0,1:T(8,128)}, f32[2,512,800]{1,2,0:T(8,128)}, f32[2,512,800]{1,2,0:T(8,128)}, bf16[2,512,800]{1,2,0:T(8,128)(2,1)S(1...) while((s32[]{:T(128)}, f32[1024,800]{0,1:T(8,128)}, ...), condition=%wide.region_5.7_spmd.clone, body=%wide.region_1.6_spmd.clone.sunk | while | flops 2527675904 | bytes 74365712 | solution.py:122
  213.2 3.0 fusion.55
  217.1 1.8 copy-done.7
  218.9 1.4 fusion.58
  220.3 1.8 copy-done.8
  222.1 1.5 multiply_dynamic-update-slice_fusion.2
  223.6 4.5 select_add_fusion.2
  228.1 3.0 fusion.55
  232.0 1.8 copy-done.7
  233.8 1.4 fusion.58
  235.3 1.8 copy-done.8
  238.4 5.4 select_add_fusion.2
  243.9 4.4 copy.95
  248.2 10.8 %scatter_custom_fusion.2 = f32[512,800]{1,0:T(8,128)S(1)} fusion(s32[1024]{0:T(1024)S(1)} %bitcast.112, f32[1024,800]{1,0:T(8,128)} %bitcast.92, f32[]{:T(128)} %constant.133.clone.1), kind=kCustom, calls=%fused_computation.49 | custom fusion | flops 819200 | bytes 1638912 | tf_op jit(solution)/shard_map/scatter-add | solution.py:135
  260.2 1.5 copy.90
  261.7 3.6 broadcast_in_dim.108
  265.3 2.8 scatter_fusion
  268.1 4.6 all-to-all-start.1
  272.8 4.9 copy.92
  277.7 6.1 reshape.276
  287.4 4.4 copy.85
  291.8 75.6 %all-to-all-done.1 = bf16[16,2,128,800]{2,3,1,0:T(8,128)(2,1)} async-done(((bf16[16,2,128,800]{2,3,1,0:T(8,128)(2,1)}), bf16[16,2,128,800]{2,3,1,0:T(8,128)(2,1)}, u32[]{:S(2)}, u32[]{:S(2)}) %all-to-all-start.1) | async-done | bytes 6553632 | tf_op jit(solution)/shard_map/all_to_all | solution.py:151
  367.4 11.0 %copy.91 = bf16[16,2,128,800]{3,2,1,0:T(8,128)(2,1)} copy(bf16[16,2,128,800]{2,3,1,0:T(8,128)(2,1)} %all-to-all-done.1) | data formatting | bytes 13107200 | tf_op jit(solution)/shard_map/all_to_all | solution.py:151
  378.5 13.6 %reshape.275 = bf16[32,102400]{1,0:T(8,128)(2,1)} reshape(bf16[16,2,128,800]{3,2,1,0:T(8,128)(2,1)} %copy.91) | data formatting | bytes 13107200 | tf_op jit(solution)/shard_map/reshape | solution.py:159
  392.1 5.1 fusion.20
  397.3 6.6 multiply_add_fusion
  403.9 10.9 %scatter_custom_fusion = f32[512,800]{1,0:T(8,128)S(1)} fusion(s32[1024]{0:T(1024)S(1)} %bitcast.113, f32[1024,400]{1,0:T(8,128)} %get-tuple-element.225, f32[]{:T(128)} %constant.164, f32[1024,400]{1,0:T(8,128)} %get-tuple-element.224, f32[]{:T(128)} %constant.133.clone.1), kind=kCustom, calls=%fused_computation.32 | custom fusion | flops 1638400 | bytes 4915208 | tf_op jit(solution)/shard_map/scatter-add | solution.py:130
  417.0 2.1 copy.93
  419.1 172.2 %all-reduce.8.cloned.1.call-done = f32[8,102400]{1,0:T(8,128)} async-done(((f32[8,102400]{1,0:T(8,128)}), f32[8,102400]{1,0:T(8,128)}) %all-reduce.8.cloned.1.call-update) | async-done | bytes 3276816 | tf_op jit(solution)/shard_map/psum | solution.py:166
  591.3 116.5 %all-reduce.6.cloned.1.call-done = f32[4,102400]{1,0:T(4,128)} async-done(((f32[4,102400]{1,0:T(4,128)}), f32[4,102400]{1,0:T(4,128)}) %all-reduce.6.cloned.1.call-update) | async-done | bytes 1638416 | tf_op jit(solution)/shard_map/psum | solution.py:37
  707.9 5.1 broadcast_multiply_fusion
  713.0 3.0 mul.159
  716.2 3.1 mul.157
  721.1 2.2 copy.94
  (109 shorter events, 24.9 us)
Async XLA Ops:
  7.2 12.1 %copy-start.3 = (bf16[4,128,800]{1,2,0:T(8,128)(2,1)S(1)}, bf16[4,128,800]{1,2,0:T(8,128)(2,1)}, u32[]{:S(2)}) copy-start(bf16[4,128,800]{1,2,0:T(8,128)(2,1)} %param.18) | copy-start | bytes 2457604
  7.2 104.3 %all-gather.2.cloned.1.call-start = ((), (), s32[]{:S(2)}) async-start(), calls=%async_computation.3 | async-start | bytes 13926400 | tf_op jit(solution)/shard_map/all_gather | solution.py:69
  10.9 257.2 %all-to-all-start = ((s32[16,1,2]{2,1,0:T(1,128)}), s32[16,1,2]{2,1,0:T(1,128)S(1)}, u32[]{:S(2)}, u32[]{:S(2)}) async-start(s32[16,1,2]{2,1,0:T(1,128)} %bitcast.13), calls=%async_computation | async-start | bytes 16384 | tf_op jit(solution)/shard_map/all_to_all | solution.py:152
  18.5 194.7 %all-reduce.4.cloned.1.call-start = ((), (), s32[]{:S(2)}) async-start(), calls=%async_computation.2 | async-start | bytes 3670016 | tf_op jit(solution)/shard_map/psum | solution.py:78
  21.5 3.8 copy-start.12
  21.5 3.9 copy-start.15
  21.5 3.9 copy-start.16
  21.5 3.9 copy-start.9
  26.1 3.1 copy-start.10
  42.4 1.8 copy-start.1
  44.2 3.1 copy-start.11
  45.4 1.9 copy-start.6
  213.2 3.1 copy-start.2
  213.2 3.9 copy-start.17
  216.2 4.1 copy-start
  216.2 2.7 copy-start.7
  220.3 1.8 copy-start.8
  228.1 3.1 copy-start.2
  228.1 3.9 copy-start.17
  231.1 4.1 copy-start
  231.1 2.7 copy-start.7
  235.2 1.8 copy-start.8
  268.1 99.3 %all-to-all-start.1 = ((bf16[16,2,128,800]{2,3,1,0:T(8,128)(2,1)}), bf16[16,2,128,800]{2,3,1,0:T(8,128)(2,1)}, u32[]{:S(2)}, u32[]{:S(2)}) async-start(bf16[16,2,128,800]{2,3,1,0:T(8,128)(2,1)} %bitcast.86), calls=%async_computation.1 | async-start | bytes 13107200 | tf_op jit(solution)/shard_map/all_to_all | solution.py:151
  272.7 318.6 %all-reduce.8.cloned.1.call-start = ((), (), s32[]{:S(2)}) async-start(), calls=%async_computation.5 | async-start | bytes 6553600 | tf_op jit(solution)/shard_map/psum | solution.py:166
  283.7 1.1 copy-start.4
  283.7 424.1 %all-reduce.6.cloned.1.call-start = ((), (), s32[]{:S(2)}) async-start(), calls=%async_computation.4 | async-start | bytes 3276800 | tf_op jit(solution)/shard_map/psum | solution.py:37
  403.9 11.1 %copy-start.13 = (f32[512]{0:T(512)S(1)}, f32[512]{0:T(512)}, u32[]{:S(2)}) copy-start(f32[512]{0:T(512)} %param.17) | copy-start | bytes 6148
  716.1 3.1 copy-start.14
  716.2 3.7 copy-start.5
Sparse Core Ops, SparseCore 0:
  10.4 101.0 all-gather.1
  114.9 98.2 all-reduce.3
  283.9 307.4 all-reduce.7
  593.6 114.2 all-reduce.5
where the time goes:
time: 731 us; the launch traced here: 730 us
  waiting for transfers between devices  509 us (70%)
  local copies, waits for them, and re-layouts  111 us (15%)
  other arithmetic  52.5 us (7%)
  matrix products  29.1 us (4%)
  between operations  14.8 us (2%)
  starting transfers between devices  12.4 us (2%)
    psum x1, waiting for transfers between devices, per_device(): neg_all = lax.psum(neg_part, ('head', 'tail'))  172 us
    psum x1, waiting for transfers between devices, head_sum(): return lax.psum(tail_grad, 'head')  117 us
    psum x1, waiting for transfers between devices, per_device(): lax.psum(own_negs.astype(jnp.float32).astype(jnp.bfloat16), 'tail')  81.5 us
    all_to_all x1, waiting for transfers between devices, per_device(): lax.all_to_all(outgoing, 'tail', split_axis=0, concat_axis=0, tiled=True)  75.6 us
    all_gather x1, waiting for transfers between devices, per_device(): partition = lax.all_gather(tail_emb, 'tail', axis=0, tiled=True)  62.8 us
  transfers between devices with their start and end apart: 6, of which 5 were waited for; matrix products, arithmetic and copies ran while one was open for 23% of the time, Pallas kernels for 0%

commit v1 on v0

--- a/solution.py
+++ b/solution.py
@@ -34,7 +34,7 @@
 
 
 def head_sum(tail_grad):
-    return lax.psum(tail_grad, "head")
+    return jnp.sum(lax.all_gather(tail_grad, "head"), axis=0)
 
 
 def per_device(

time: 731 us -> 837 us (1.15); the launches traced: 730 us -> 826 us
  waiting for transfers between devices: 509 us -> 599 us
  other arithmetic: 52.5 us -> 61.4 us
    psum x1 -> x0, waiting for transfers between devices: 117 us -> none  [head_sum(): return lax.psum(tail_grad, 'head')]
    all_gather x0 -> x1, waiting for transfers between devices: none -> 103 us  [head_sum(): return jnp.sum(lax.all_gather(tail_grad, 'head'), axis=0)]
    psum x1, waiting for transfers between devices: 172 us -> 260 us  [per_device(): neg_all = lax.psum(neg_part, ('head', 'tail'))]
    all_to_all x1, waiting for transfers between devices: 75.6 us -> 91.5 us  [per_device(): lax.all_to_all(outgoing, 'tail', split_axis=0, concat_axis=0, tiled=True)]
    reduce_sum x0 -> x1, other arithmetic: none -> 9.63 us  [head_sum(): return jnp.sum(lax.all_gather(tail_grad, 'head'), axis=0)]
  transfers between devices with their start and end apart: 6 -> 6, of which waited for: 5 -> 5; matrix products, arithmetic and copies ran while one was open for 23% -> 17% of each run, Pallas kernels for 0% -> 0%
where the time goes in v1:
time: 837 us; the launch traced here: 826 us
  waiting for transfers between devices  599 us (72%)
  local copies, waits for them, and re-layouts  116 us (14%)
  other arithmetic  61.4 us (7%)
  matrix products  22.6 us (3%)
  between operations  15 us (2%)
  starting transfers between devices  12.4 us (1%)
    psum x1, waiting for transfers between devices, per_device(): neg_all = lax.psum(neg_part, ('head', 'tail'))  260 us
    all_gather x1, waiting for transfers between devices, head_sum(): return jnp.sum(lax.all_gather(tail_grad, 'head'), axis=0)  103 us
    all_to_all x1, waiting for transfers between devices, per_device(): lax.all_to_all(outgoing, 'tail', split_axis=0, concat_axis=0, tiled=True)  91.5 us
    psum x1, waiting for transfers between devices, per_device(): lax.psum(own_negs.astype(jnp.float32).astype(jnp.bfloat16), 'tail')  81.5 us
    all_gather x1, waiting for transfers between devices, per_device(): partition = lax.all_gather(tail_emb, 'tail', axis=0, tiled=True)  62.8 us
  transfers between devices with their start and end apart: 6, of which 5 were waited for; matrix products, arithmetic and copies ran while one was open for 17% of the time, Pallas kernels for 0%

profile of v1, /device:TPU:1, one launch (start us, length us, event | category | flops | bytes accessed | tf_op | source)
XLA Modules:
  0.0 826.1 jit_solution(9198306023450606556)
XLA Ops:
  10.9 7.6 all-to-all-start
  20.1 1.4 select_select_fusion
  21.5 3.8 copy.82
  26.1 3.1 copy.79
  29.3 5.3 gather_fusion.3
  34.5 5.3 gather_fusion
  39.8 2.5 select_convert_fusion
  42.4 1.5 subtract_convert_fusion
  48.8 62.8 %all-gather.5.cloned.1.call-done = bf16[64,128,800]{1,2,0:T(8,128)(2,1)} async-done(((bf16[4,128,800]{1,2,0:T(8,128)(2,1)}), bf16[64,128,800]{1,2,0:T(8,128)(2,1)}) %all-gather.5.cloned.1.call-update) | async-done | bytes 13107216 | tf_op jit(solution)/shard_map/all_gather | solution.py:69
  111.5 5.4 gather_fusion.2
  119.6 5.3 gather_fusion.4
  124.9 3.3 broadcast_select_fusion
  128.2 3.5 copy.84
  131.7 81.5 %all-reduce.3.cloned.1.call-done = bf16[1024,800]{1,0:T(8,128)(2,1)} async-done(((bf16[1024,800]{1,0:T(8,128)(2,1)}), bf16[1024,800]{1,0:T(8,128)(2,1)}) %all-reduce.3.cloned.1.call-update) | async-done | bytes 1638416 | tf_op jit(solution)/shard_map/psum | solution.py:78
  213.2 24.3 %while.17 = (s32[]{:T(128)}, f32[1024,800]{0,1:T(8,128)}, f32[2,512,800]{1,2,0:T(8,128)}, f32[2,512,800]{1,2,0:T(8,128)}, bf16[2,512,800]{1,2,0:T(8,128)(2,1)S(1...) while((s32[]{:T(128)}, f32[1024,800]{0,1:T(8,128)}, ...), condition=%wide.region_5.7_spmd.clone, body=%wide.region_1.6_spmd.clone.sunk | while | flops 2527675904 | bytes 118405488 | solution.py:122
  213.2 3.0 fusion.54
  218.1 1.9 select_add_fusion.2
  220.6 1.4 fusion.57
  223.7 1.6 copy-done.11
  225.3 3.0 fusion.54
  230.2 1.9 select_add_fusion.2
  232.7 1.4 fusion.57
  234.1 1.4 copy-done.10
  235.8 1.6 copy-done.11
  237.4 4.4 copy.95
  241.8 11.1 %scatter_custom_fusion.2 = f32[512,800]{1,0:T(8,128)S(1)} fusion(s32[1024]{0:T(1024)S(1)} %bitcast.114, f32[1024,800]{1,0:T(8,128)} %bitcast.94, f32[]{:T(128)} %constant.133.clone.1), kind=kCustom, calls=%fused_computation.50 | custom fusion | flops 819200 | bytes 1638912 | tf_op jit(solution)/shard_map/scatter-add | solution.py:135
  253.9 1.5 copy.90
  255.5 3.6 broadcast_in_dim.108
  259.1 2.8 scatter_fusion
  261.8 4.6 all-to-all-start.1
  267.8 91.5 %all-to-all-done.1 = bf16[16,2,128,800]{2,3,1,0:T(8,128)(2,1)} async-done(((bf16[16,2,128,800]{2,3,1,0:T(8,128)(2,1)}), bf16[16,2,128,800]{2,3,1,0:T(8,128)(2,1)}, u32[]{:S(2)}, u32[]{:S(2)}) %all-to-all-start.1) | async-done | bytes 6553632 | tf_op jit(solution)/shard_map/all_to_all | solution.py:151
  359.3 11.0 %copy.91 = bf16[16,2,128,800]{3,2,1,0:T(8,128)(2,1)} copy(bf16[16,2,128,800]{2,3,1,0:T(8,128)(2,1)} %all-to-all-done.1) | data formatting | bytes 13107200 | tf_op jit(solution)/shard_map/all_to_all | solution.py:151
  370.3 13.6 %reshape.275 = bf16[32,102400]{1,0:T(8,128)(2,1)} reshape(bf16[16,2,128,800]{3,2,1,0:T(8,128)(2,1)} %copy.91) | data formatting | bytes 13107200 | tf_op jit(solution)/shard_map/reshape | solution.py:159
  383.9 5.1 convolution_bitcast_fusion
  389.1 5.0 copy.92
  394.2 6.0 reshape.276
  402.6 4.9 copy.85
  407.5 6.6 multiply_add_fusion
  414.1 10.9 %scatter_custom_fusion = f32[512,800]{1,0:T(8,128)S(1)} fusion(s32[1024]{0:T(1024)S(1)} %bitcast.115, f32[1024,400]{1,0:T(8,128)} %get-tuple-element.225, f32[]{:T(128)} %constant.164, f32[1024,400]{1,0:T(8,128)} %get-tuple-element.224, f32[]{:T(128)} %constant.133.clone.1), kind=kCustom, calls=%fused_computation.33 | custom fusion | flops 1638400 | bytes 4915208 | tf_op jit(solution)/shard_map/scatter-add | solution.py:130
  427.1 2.3 copy.93
  429.5 102.5 %all-gather.7.cloned.1.call-done = f32[16,4,102400]{2,1,0:T(4,128)} async-done(((f32[1,4,102400]{2,1,0:T(4,128)}), f32[16,4,102400]{2,1,0:T(4,128)}) %all-gather.7.cloned.1.call-update) | async-done | bytes 26214416 | tf_op jit(solution)/shard_map/all_gather | solution.py:37
  532.0 9.6 %reduce_sum.65 = f32[4,102400]{1,0:T(4,128)S(1)} reduce(f32[16,4,102400]{2,1,0:T(4,128)} %all-gather.7.cloned.1.call-done, f32[]{:T(128)} %constant.133.clone.1), dimensions={0}, to_apply=%region_12.14 | reduce | flops 6144000 | bytes 27852804 | tf_op jit(solution)/shard_map/reduce_sum | solution.py:37
  541.6 259.7 %all-reduce.5.cloned.1.call-done = f32[8,102400]{1,0:T(8,128)} async-done(((f32[8,102400]{1,0:T(8,128)}), f32[8,102400]{1,0:T(8,128)}) %all-reduce.5.cloned.1.call-update) | async-done | bytes 3276816 | tf_op jit(solution)/shard_map/psum | solution.py:166
  801.4 4.9 broadcast_multiply_fusion
  806.3 3.0 mul.157
  809.3 4.3 mul.159
  813.6 1.7 reduce_sum.66
  817.2 2.2 copy.94
  (122 shorter events, 28.6 us)
Async XLA Ops:
  7.2 12.1 %copy-start.2 = (bf16[4,128,800]{1,2,0:T(8,128)(2,1)S(1)}, bf16[4,128,800]{1,2,0:T(8,128)(2,1)}, u32[]{:S(2)}) copy-start(bf16[4,128,800]{1,2,0:T(8,128)(2,1)} %param.18) | copy-start | bytes 2457604
  7.2 104.3 %all-gather.5.cloned.1.call-start = ((), (), s32[]{:S(2)}) async-start(), calls=%async_computation.3 | async-start | bytes 13926400 | tf_op jit(solution)/shard_map/all_gather | solution.py:69
  10.9 250.9 %all-to-all-start = ((s32[16,1,2]{2,1,0:T(1,128)}), s32[16,1,2]{2,1,0:T(1,128)S(1)}, u32[]{:S(2)}, u32[]{:S(2)}) async-start(s32[16,1,2]{2,1,0:T(1,128)} %bitcast.13), calls=%async_computation | async-start | bytes 16384 | tf_op jit(solution)/shard_map/all_to_all | solution.py:152
  18.5 194.7 %all-reduce.3.cloned.1.call-start = ((), (), s32[]{:S(2)}) async-start(), calls=%async_computation.2 | async-start | bytes 3670016 | tf_op jit(solution)/shard_map/psum | solution.py:78
  21.5 3.9 copy-start.15
  21.5 3.9 copy-start.18
  21.5 3.9 copy-start.19
  21.5 3.9 copy-start.12
  26.1 3.1 copy-start.13
  42.4 1.9 copy-start
  44.2 3.1 copy-start.14
  45.4 1.9 copy-start.5
  213.2 3.0 copy-start.1
  216.2 1.9 copy-start.6
  218.1 1.9 copy-start.8
  218.1 2.5 copy-start.20
  220.0 2.0 copy-start.7
  220.6 2.8 copy-start.10
  222.0 1.7 copy-start.9
  223.6 1.7 copy-start.11
  225.3 3.0 copy-start.1
  228.3 1.9 copy-start.6
  230.2 1.9 copy-start.8
  230.2 2.5 copy-start.20
  232.1 2.0 copy-start.7
  232.7 2.8 copy-start.10
  234.1 1.7 copy-start.9
  235.7 1.7 copy-start.11
  261.8 97.5 %all-to-all-start.1 = ((bf16[16,2,128,800]{2,3,1,0:T(8,128)(2,1)}), bf16[16,2,128,800]{2,3,1,0:T(8,128)(2,1)}, u32[]{:S(2)}, u32[]{:S(2)}) async-start(bf16[16,2,128,800]{2,3,1,0:T(8,128)(2,1)} %bitcast.88), calls=%async_computation.1 | async-start | bytes 13107200 | tf_op jit(solution)/shard_map/all_to_all | solution.py:151
  266.5 265.5 %all-gather.7.cloned.1.call-start = ((), (), s32[]{:S(2)}) async-start(), calls=%async_computation.5 | async-start | bytes 27852800 | tf_op jit(solution)/shard_map/all_gather | solution.py:37
  389.1 412.3 %all-reduce.5.cloned.1.call-start = ((), (), s32[]{:S(2)}) async-start(), calls=%async_computation.4 | async-start | bytes 6553600 | tf_op jit(solution)/shard_map/psum | solution.py:166
  400.1 1.1 copy-start.3
  414.1 11.1 %copy-start.16 = (f32[512]{0:T(512)S(1)}, f32[512]{0:T(512)}, u32[]{:S(2)}) copy-start(f32[512]{0:T(512)} %param.17) | copy-start | bytes 6148
  809.3 6.0 copy-start.17
  809.3 6.6 copy-start.4
Sparse Core Ops, SparseCore 0:
  10.4 101.0 all-gather.4
  114.9 98.2 all-reduce.2
  389.2 142.7 all-gather.6
  537.4 263.9 all-reduce.4
